TPU v7x, 256 devices: a whole 4x4x8 slice. The times are simulated.
256 devices in a mesh: section: 2 (over z_hi), gy: 32 (over z_lo, x, core), gz: 4 (over y).
Axes of the slice: x: 4, y: 4, z: 8 (z_hi: 2, z_lo: 4; z = z_hi * 4 + z_lo), core: 2. Of those that a mesh axis runs over, the one named last changes fastest.
Arguments:
- inflow: float32 [2, 64, 2, 64, 512], P(None, None, None, 'gy', 'gz'), may hold values from -6 to 6
- weights: float32 [4, 27, 64, 64], P('section'), may hold values from -0.15625 to 0.15625
- biases: float32 [4, 64], P('section'), may hold values from -3 to 3
- cotangent: float32 [2, 64, 2, 64, 512], P(None, None, None, 'gy', 'gz'), may hold values from -6 to 6
Outputs:
- section_out: float32 [2, 2, 64, 2, 64, 512], P('section', None, None, None, 'gy', 'gz')
- section_grad: float32 [2, 2, 64, 2, 64, 512], P('section', None, None, None, 'gy', 'gz')
- weight_grad: float32 [4, 27, 64, 64], P('section')
- bias_grad: float32 [4, 64], P('section')
All inputs are finite; a program needn't handle non-finite values.
Results may differ from a plain program's by a relative error of at most 0.0001.
Values sent between devices are 32-bit elements; how exact they have to be, the bound alone decides.
A program may use at most 128 MiB of HBM per device.

v0:
```python
import math
import jax
import jax.numpy as jnp
from jax import lax
from jax.sharding import PartitionSpec as P


def extended(block, sides, width):
    for axis, dim in sides:
        count = lax.axis_size(axis)
        forward = [(i, i + 1) for i in range(count - 1)]
        backward = [(target, source) for source, target in forward]
        low = lax.ppermute(
            lax.slice_in_dim(block, block.shape[dim] - width, None, axis=dim), axis, forward
        )
        high = lax.ppermute(lax.slice_in_dim(block, 0, width, axis=dim), axis, backward)
        block = jnp.concatenate([low, block, high], axis=dim)
    return block


def passed_along(block, axis, distance):
    devices = range(lax.axis_size(axis))
    route = [(i - distance, i) for i in devices if i - distance in devices]
    return lax.ppermute(block, axis, route)


def stacked_taps(padded, out_sizes, flipped):
    size_x, size_y, size_z = out_sizes
    pieces = []
    for offset in range(27):
        start_x, start_y, start_z = (offset // 9, offset // 3 % 3, offset % 3)
        if flipped:
            start_x, start_y, start_z = (2 - start_x, 2 - start_y, 2 - start_z)
        pieces.append(
            padded[
                :,
                start_x : start_x + size_x,
                start_y : start_y + size_y,
                start_z : start_z + size_z,
            ]
        )
    return jnp.stack(pieces)


def convolve(weight, padded, out_sizes):
    return jnp.einsum(
        "toc,tcxyz->oxyz",
        weight,
        stacked_taps(padded, out_sizes, False),
        precision=lax.Precision.HIGHEST,
    )


def face_rim(values):
    rimmed = extended(values, (("gy", 2), ("gz", 3)), 1)
    return jnp.pad(rimmed, ((0, 0), (1, 1), (0, 0), (0, 0)))


def slope_rim(values):
    rimmed = extended(values, (("gy", 2), ("gz", 3)), 1)
    return jnp.pad(rimmed, ((0, 0), (1, 1), (0, 0), (0, 0)))


def section_forward(weights, biases, current, extents):
    stored = []
    for layer_index in range(weights.shape[0]):
        padded = face_rim(current)
        pre_act = (
            convolve(weights[layer_index], padded, extents)
            + biases[layer_index][:, None, None, None]
        )
        stored.append((padded, pre_act))
        current = jax.nn.silu(pre_act)
    return (stored, current)


def per_device(inflow, weights, biases, cotangent):
    highest = lax.Precision.HIGHEST
    first_section = lax.axis_index("section") == 0
    micro_count = inflow.shape[0]
    layer_count = weights.shape[0]
    extents = inflow.shape[2:]
    blank = jnp.zeros(inflow.shape[1:], jnp.float32)
    received = blank
    stored_all = []
    produced = []
    for step_index in range(micro_count + 1):
        own_input = inflow[step_index] if step_index < micro_count else blank
        current = jnp.where(first_section, own_input, received)
        stored, current = section_forward(weights, biases, current, extents)
        stored_all.append(stored)
        produced.append(current)
        if step_index < micro_count:
            received = passed_along(current, "section", 1)
    section_out = jnp.stack(
        [
            jnp.where(first_section, produced[micro], produced[micro + 1])
            for micro in range(micro_count)
        ]
    )
    cell_count = (
        micro_count
        * extents[0]
        * extents[1]
        * lax.axis_size("gy")
        * extents[2]
        * lax.axis_size("gz")
    )
    grad_scale = 1.0 / math.sqrt(cell_count)
    weight_grads = [jnp.zeros(weights.shape[1:], jnp.float32) for layer_index in range(layer_count)]
    bias_grads = [jnp.zeros(biases.shape[1:], jnp.float32) for layer_index in range(layer_count)]
    returned = blank
    collected = []
    for step_index in range(micro_count + 1):
        later = micro_count - 1 - step_index
        own_grad = cotangent[later] if later >= 0 else blank
        gradient = jnp.where(first_section, returned, own_grad)
        stored = stored_all[micro_count - step_index]
        for layer_index in reversed(range(layer_count)):
            padded, pre_act = stored[layer_index]
            sigmoid_value = jax.nn.sigmoid(pre_act)
            slope_grad = gradient * sigmoid_value * (1.0 + pre_act * (1.0 - sigmoid_value))
            weight_grads[layer_index] = weight_grads[layer_index] + jnp.einsum(
                "oxyz,tcxyz->toc",
                slope_grad,
                stacked_taps(padded, extents, False),
                precision=highest,
            )
            bias_grads[layer_index] = bias_grads[layer_index] + jnp.sum(slope_grad, axis=(1, 2, 3))
            gradient = jnp.einsum(
                "toc,toxyz->cxyz",
                weights[layer_index],
                stacked_taps(slope_rim(slope_grad), extents, True),
                precision=highest,
            )
        collected.append(gradient)
        if step_index < micro_count:
            returned = passed_along(gradient, "section", -1)
    section_grad = jnp.stack(
        [
            jnp.where(
                first_section, collected[micro_count - micro], collected[micro_count - 1 - micro]
            )
            for micro in range(micro_count)
        ]
    )
    weight_total, bias_total = lax.psum(
        (jnp.stack(weight_grads) * grad_scale, jnp.stack(bias_grads) * grad_scale), ("gy", "gz")
    )
    return (section_out[None], section_grad[None], weight_total, bias_total)


def solution(mesh):
    return jax.shard_map(
        per_device,
        mesh=mesh,
        in_specs=(
            P(None, None, None, "gy", "gz"),
            P("section", None, None, None),
            P("section", None),
            P(None, None, None, "gy", "gz"),
        ),
        out_specs=(
            P("section", None, None, None, "gy", "gz"),
            P("section", None, None, None, "gy", "gz"),
            P("section", None, None, None),
            P("section", None),
        ),
        check_vma=False,
    )
```

profile of v0, /device:TPU:8, one launch (start us, length us, event | category | flops | bytes accessed | tf_op | source)
XLA Modules:
  0.0 1630.1 jit_solution(7726312461387545481)
XLA Ops:
  23.6 3.8 collective-permute-done.3
  37.2 4.1 collective-permute-done.5
  59.0 9.1 collective-permute-start.8
  75.4 4.7 collective-permute-done.10
  82.2 4.2 collective-permute-start.12
  96.2 3.8 collective-permute-start.13
  101.3 4.0 collective-permute-done.14
  122.1 8.2 collective-permute-start.17
  162.3 4.1 collective-permute-done.23
  168.5 4.4 collective-permute-start.25
  182.8 3.8 collective-permute-start.26
  193.3 3.9 collective-permute-start.29
  207.2 3.8 collective-permute-start.30
  212.2 3.8 collective-permute-done.31
  218.2 3.9 collective-permute-start.33
  233.2 10.2 collective-permute-done.34
  247.7 4.6 collective-permute-done.36
  278.4 3.7 collective-permute-start.42
  296.9 7.1 collective-permute-done.43
  316.8 4.2 collective-permute-start.47
  335.1 3.8 collective-permute-start.48
  345.9 3.9 collective-permute-start.51
  349.8 333.4 %psum.15 = f32[2,64]{1,0:T(2,128)} all-reduce(f32[2,64]{1,0:T(2,128)S(1)} %maximum_multiply_fusion.1), channel_id=1, replica_groups=mesh['section'=2,'gy'=32,'gz'=4] {'gy','gz'}, use_global_device_ids=true, to_apply=%region_7.8 | all-reduce | flops 128 | bytes 1024 | tf_op jit(solution)/shard_map/psum | solution.py:147
  688.9 931.3 %all-reduce.14.cloned.1.call-done = f32[2,27,64,64]{2,3,1,0:T(8,128)} async-done(((f32[2,27,64,64]{2,3,1,0:T(8,128)}), f32[2,27,64,64]{2,3,1,0:T(8,128)}) %all-reduce.14.cloned.1.call-update) | async-done | bytes 884752 | tf_op jit(solution)/shard_map/psum | solution.py:147
  (506 shorter events, 240.5 us)
Async XLA Ops:
  7.2 1613.0 %all-reduce.14.cloned.1.call-start = ((), (), s32[]{:S(2)}) async-start(), calls=%async_computation | async-start | bytes 3538944 | tf_op jit(solution)/shard_map/psum | solution.py:147
  18.1 9.3 collective-permute-start.3
  41.4 9.0 collective-permute-start.6
  44.6 9.3 collective-permute-start.7
  59.0 12.4 collective-permute-start.8
  80.2 9.0 collective-permute-start.11
  82.2 9.0 collective-permute-start.12
  105.5 9.0 collective-permute-start.15
  107.7 9.3 collective-permute-start.16
  122.1 11.4 collective-permute-start.17
  141.0 9.0 collective-permute-start.20
  143.2 9.3 collective-permute-start.21
  216.2 9.0 collective-permute-start.32
  218.2 9.1 collective-permute-start.33
  231.9 11.5 collective-permute-start.34
  252.4 9.0 collective-permute-start.37
  254.8 9.3 collective-permute-start.38
  276.3 9.0 collective-permute-start.41
  278.4 9.3 collective-permute-start.42
  292.4 11.6 collective-permute-start.43
  314.8 9.0 collective-permute-start.46
  316.8 9.0 collective-permute-start.47
  344.0 339.3 %collective-permute-start.50 = (f32[64,2,4,1]{3,0,2,1:T(8,128)S(1)}, f32[64,2,4,1]{3,0,2,1:T(8,128)S(1)}, u32[]{:S(2)}, u32[]{:S(2)}) collective-permute-start(f32[64,2,4,1]{3,0,2,1:T(8,128)S(1)} %get-tuple-element.22), channel_id=1, source_target_pairs={{0,1},{1,2},{2,3},{4,5},{5,6},{6,7},{8,9},{9,10},{10,11},{12,13},{... | collective-permute-start | bytes 6152 | tf_op jit(solution)/shard_map/ppermute | solution.py:13
  345.9 337.4 %collective-permute-start.51 = (f32[64,2,4,1]{3,0,2,1:T(8,128)S(1)}, f32[64,2,4,1]{3,0,2,1:T(8,128)S(1)}, u32[]{:S(2)}, u32[]{:S(2)}) collective-permute-start(f32[64,2,4,1]{3,0,2,1:T(8,128)S(1)} %get-tuple-element.23), channel_id=1, source_target_pairs={{1,0},{2,1},{3,2},{5,4},{6,5},{7,6},{9,8},{10,9},{11,10},{13,12},{... | collective-permute-start | bytes 6152 | tf_op jit(solution)/shard_map/ppermute | solution.py:16
  (31 other events, 182.5 us)
Sparse Core Ops, SparseCore 0:
  335.3 1284.8 all-reduce.13
where the time goes:
time: 1640 us; the launch traced here: 1630 us
  waiting for transfers between devices  1050 us (64%)
  blocking collectives  333 us (20%)
  starting transfers between devices  144 us (9%)
  matrix products  46.1 us (3%)
  local copies, waits for them, and re-layouts  22.3 us (1%)
  between operations  18 us (1%)
    psum x1, waiting for transfers between devices, per_device(): lax.psum((jnp.stack(weight_grads) * grad_scale, jnp.stack(bias_grads) * g...  931 us
    psum x1, blocking collectives, per_device(): lax.psum((jnp.stack(weight_grads) * grad_scale, jnp.stack(bias_grads) * g...  333 us
    ppermute x24, waiting for transfers between devices, extended(): lax.ppermute(lax.slice_in_dim(block, 0, width, axis=dim), axis, backward)  67.7 us
    ppermute x24, starting transfers between devices, extended(): lax.ppermute(lax.slice_in_dim(block, block.shape[dim] - width, None, axis...  64.7 us
    ppermute x24, starting transfers between devices, extended(): lax.ppermute(lax.slice_in_dim(block, 0, width, axis=dim), axis, backward)  59.7 us
  transfers between devices with their start and end apart: 53, of which 38 were waited for; matrix products, arithmetic and copies ran while one was open for 1% of the time, Pallas kernels for 0%

commit v1 on v0

--- a/solution.py
+++ b/solution.py
@@ -1,8 +1,16 @@
+import functools
 import math
 import jax
 import jax.numpy as jnp
 from jax import lax
 from jax.sharding import PartitionSpec as P
+
+
+def unite_floor(local_array, group_axis, comm_axis):
+    return jax.lax.psum(jax.lax.psum(local_array, group_axis), comm_axis)
+
+
+state_corner = functools.partial(unite_floor, group_axis="gy", comm_axis="gz")
 
 
 def extended(block, sides, width):
@@ -144,8 +152,8 @@
             for micro in range(micro_count)
         ]
     )
-    weight_total, bias_total = lax.psum(
-        (jnp.stack(weight_grads) * grad_scale, jnp.stack(bias_grads) * grad_scale), ("gy", "gz")
+    weight_total, bias_total = state_corner(
+        (jnp.stack(weight_grads) * grad_scale, jnp.stack(bias_grads) * grad_scale)
     )
     return (section_out[None], section_grad[None], weight_total, bias_total)
 

time: 1640 us -> 698 us (0.43)
  waiting for transfers between devices: 1050 us -> 340 us
  blocking collectives: 333 us -> 77.7 us
    psum x1 -> x2, waiting for transfers between devices: 931 us -> 222 us  [unite_floor(): return jax.lax.psum(jax.lax.psum(local_array, group_axis), comm_axis)]
    psum x1 -> x2, blocking collectives: 333 us -> 77.7 us  [unite_floor(): return jax.lax.psum(jax.lax.psum(local_array, group_axis), comm_axis)]
  transfers between devices with their start and end apart: 53 -> 54, of which waited for: 38 -> 39; matrix products, arithmetic and copies ran while one was open for 1% -> 6% of each run, Pallas kernels for 0% -> 0%
where the time goes in v1:
time: 698 us; the launch traced here: 688 us
  waiting for transfers between devices  340 us (49%)
  starting transfers between devices  145 us (21%)
  blocking collectives  77.7 us (11%)
  matrix products  48.1 us (7%)
  local copies, waits for them, and re-layouts  34.8 us (5%)
  other arithmetic  24.8 us (4%)
  between operations  17.8 us (3%)
    psum x2, waiting for transfers between devices, unite_floor(): return jax.lax.psum(jax.lax.psum(local_array, group_axis), comm_axis)  222 us
    psum x2, blocking collectives, unite_floor(): return jax.lax.psum(jax.lax.psum(local_array, group_axis), comm_axis)  77.7 us
    ppermute x24, waiting for transfers between devices, extended(): lax.ppermute(lax.slice_in_dim(block, 0, width, axis=dim), axis, backward)  67.8 us
    ppermute x24, starting transfers between devices, extended(): lax.ppermute(lax.slice_in_dim(block, block.shape[dim] - width, None, axis...  64.7 us
    ppermute x24, starting transfers between devices, extended(): lax.ppermute(lax.slice_in_dim(block, 0, width, axis=dim), axis, backward)  59.7 us
    unnamed x222, local copies, waits for them, and re-layouts  30 us
    ppermute x24, waiting for transfers between devices, extended(): lax.ppermute(lax.slice_in_dim(block, block.shape[dim] - width, None, axis...  27 us
    ppermute x4, waiting for transfers between devices, passed_along(): return lax.ppermute(block, axis, route)  23.7 us
  transfers between devices with their start and end apart: 54, of which 39 were waited for; matrix products, arithmetic and copies ran while one was open for 6% of the time, Pallas kernels for 0%

profile of v1, /device:TPU:8, one launch (start us, length us, event | category | flops | bytes accessed | tf_op | source)
XLA Modules:
  0.0 687.9 jit_solution(15714478837259856900)
XLA Ops:
  23.6 3.8 collective-permute-done.3
  37.2 4.1 collective-permute-done.5
  59.0 9.1 %collective-permute-start.8 = (f32[64,2,2,128]{3,0,2,1:T(8,128)S(1)}, f32[64,2,2,128]{3,0,2,1:T(8,128)S(1)}, u32[]{:S(2)}, u32[]{:S(2)}) collective-permute-start(f32[64,2,2,128]{3,0,2,1:T(8,128)S(1)} %bitcast_multiply_fusion.12), channel_id=1, source_target_pairs={{0,128},{1,129},{2,130},{3,131},{4,132},{5,133},{6,134},{7,135},{8... | collective-permute-start | bytes 393224 | tf_op jit(solution)/shard_map/ppermute | solution.py:32
  75.4 4.7 collective-permute-done.10
  82.2 4.2 collective-permute-start.12
  101.3 4.0 collective-permute-done.14
  122.2 8.2 %collective-permute-start.17 = (f32[64,2,2,128]{3,0,2,1:T(8,128)S(1)}, f32[64,2,2,128]{3,0,2,1:T(8,128)S(1)}, u32[]{:S(2)}, u32[]{:S(2)}) collective-permute-start(f32[64,2,2,128]{3,0,2,1:T(8,128)S(1)} %get-tuple-element.21), channel_id=1, source_target_pairs={{0,128},{1,129},{2,130},{3,131},{4,132},{5,133},{6,134},{7,135},{8... | collective-permute-start | bytes 393224 | tf_op jit(solution)/shard_map/ppermute | solution.py:32
  162.4 4.1 collective-permute-done.23
  168.5 4.4 collective-permute-start.25
  193.3 3.9 collective-permute-start.29
  207.2 3.8 collective-permute-start.30
  212.3 3.8 collective-permute-done.31
  218.2 3.9 collective-permute-start.33
  233.2 10.2 %collective-permute-done.34 = f32[64,2,2,128]{3,0,2,1:T(8,128)S(1)} collective-permute-done((f32[64,2,2,128]{3,0,2,1:T(8,128)S(1)}, f32[64,2,2,128]{3,0,2,1:T(8,128)S(1)}, u32[]{:S(2)}, u32[]{:S(2)}) %collective-permute-start.34) | collective-permute-done | bytes 131104 | tf_op jit(solution)/shard_map/ppermute | solution.py:32
  247.7 4.6 collective-permute-done.36
  296.9 7.0 %collective-permute-done.43 = f32[64,2,2,128]{3,0,2,1:T(8,128)S(1)} collective-permute-done((f32[64,2,2,128]{3,0,2,1:T(8,128)S(1)}, f32[64,2,2,128]{3,0,2,1:T(8,128)S(1)}, u32[]{:S(2)}, u32[]{:S(2)}) %collective-permute-start.43) | collective-permute-done | bytes 131104 | tf_op jit(solution)/shard_map/ppermute | solution.py:32
  316.8 4.2 collective-permute-start.47
  335.2 3.8 collective-permute-start.48
  345.9 3.9 collective-permute-start.51
  349.9 69.7 %psum.30 = f32[2,64]{1,0:T(2,128)S(1)} all-reduce(f32[2,64]{1,0:T(2,128)S(1)} %maximum_multiply_fusion.1), channel_id=1, replica_groups=mesh['section'=2,'gy'=32,'gz'=4] {'gy'}, use_global_device_ids=true, to_apply=%region_8.9 | all-reduce | flops 128 | bytes 1024 | tf_op jit(solution)/shard_map/psum | solution.py:10
  419.6 7.9 %psum.31 = f32[2,64]{1,0:T(2,128)} all-reduce(f32[2,64]{1,0:T(2,128)S(1)} %psum.30), channel_id=1, replica_groups=mesh['section'=2,'gy'=32,'gz'=4] {'gz'}, use_global_device_ids=true, to_apply=%region_9.10 | all-reduce | flops 128 | bytes 1024 | tf_op jit(solution)/shard_map/psum | solution.py:10
  450.5 168.9 %all-reduce.15.cloned.1.call-done = f32[2,27,64,64]{2,3,1,0:T(8,128)} async-done(((f32[2,27,64,64]{2,3,1,0:T(8,128)}), f32[2,27,64,64]{2,3,1,0:T(8,128)}) %all-reduce.15.cloned.1.call-update) | async-done | bytes 884752 | tf_op jit(solution)/shard_map/psum | solution.py:10
  620.1 4.1 fusion
  625.3 52.7 %all-reduce.17.cloned.1.call-done = f32[2,27,64,64]{2,3,1,0:T(8,128)} async-done(((f32[2,27,64,64]{2,3,1,0:T(8,128)}), f32[2,27,64,64]{2,3,1,0:T(8,128)}) %all-reduce.17.cloned.1.call-update) | async-done | bytes 884752 | tf_op jit(solution)/shard_map/psum | solution.py:10
  (514 shorter events, 271.0 us)
Async XLA Ops:
  7.2 612.3 %all-reduce.15.cloned.1.call-start = ((), (), s32[]{:S(2)}) async-start(), calls=%async_computation | async-start | bytes 3538944 | tf_op jit(solution)/shard_map/psum | solution.py:10
  14.6 9.0 %collective-permute-start.2 = (f32[64,2,4,1]{3,0,2,1:T(8,128)S(1)}, f32[64,2,4,1]{3,0,2,1:T(8,128)S(1)}, u32[]{:S(2)}, u32[]{:S(2)}) collective-permute-start(f32[64,2,4,1]{3,0,2,1:T(8,128)S(1)} %get-tuple-element.48), channel_id=1, source_target_pairs={{0,1},{1,2},{2,3},{4,5},{5,6},{6,7},{8,9},{9,10},{10,11},{12,13},{... | collective-permute-start | bytes 6152 | tf_op jit(solution)/shard_map/ppermute | solution.py:21
  18.1 9.3 %collective-permute-start.3 = (f32[64,2,4,1]{3,0,2,1:T(8,128)S(1)}, f32[64,2,4,1]{3,0,2,1:T(8,128)S(1)}, u32[]{:S(2)}, u32[]{:S(2)}) collective-permute-start(f32[64,2,4,1]{3,0,2,1:T(8,128)S(1)} %get-tuple-element.49), channel_id=1, source_target_pairs={{1,0},{2,1},{3,2},{5,4},{6,5},{7,6},{9,8},{10,9},{11,10},{13,12},{... | collective-permute-start | bytes 6152 | tf_op jit(solution)/shard_map/ppermute | solution.py:24
  41.4 9.0 %collective-permute-start.6 = (f32[64,2,4,1]{3,0,2,1:T(8,128)S(1)}, f32[64,2,4,1]{3,0,2,1:T(8,128)S(1)}, u32[]{:S(2)}, u32[]{:S(2)}) collective-permute-start(f32[64,2,4,1]{3,0,2,1:T(8,128)S(1)} %get-tuple-element.46), channel_id=1, source_target_pairs={{0,1},{1,2},{2,3},{4,5},{5,6},{6,7},{8,9},{9,10},{10,11},{12,13},{... | collective-permute-start | bytes 6152 | tf_op jit(solution)/shard_map/ppermute | solution.py:21
  44.6 9.3 %collective-permute-start.7 = (f32[64,2,4,1]{3,0,2,1:T(8,128)S(1)}, f32[64,2,4,1]{3,0,2,1:T(8,128)S(1)}, u32[]{:S(2)}, u32[]{:S(2)}) collective-permute-start(f32[64,2,4,1]{3,0,2,1:T(8,128)S(1)} %get-tuple-element.47), channel_id=1, source_target_pairs={{1,0},{2,1},{3,2},{5,4},{6,5},{7,6},{9,8},{10,9},{11,10},{13,12},{... | collective-permute-start | bytes 6152 | tf_op jit(solution)/shard_map/ppermute | solution.py:24
  59.0 12.4 %collective-permute-start.8 = (f32[64,2,2,128]{3,0,2,1:T(8,128)S(1)}, f32[64,2,2,128]{3,0,2,1:T(8,128)S(1)}, u32[]{:S(2)}, u32[]{:S(2)}) collective-permute-start(f32[64,2,2,128]{3,0,2,1:T(8,128)S(1)} %bitcast_multiply_fusion.12), channel_id=1, source_target_pairs={{0,128},{1,129},{2,130},{3,131},{4,132},{5,133},{6,134},{7,135},{8... | collective-permute-start | bytes 393224 | tf_op jit(solution)/shard_map/ppermute | solution.py:32
  80.2 9.0 %collective-permute-start.11 = (f32[64,2,4,1]{3,0,2,1:T(8,128)S(1)}, f32[64,2,4,1]{3,0,2,1:T(8,128)S(1)}, u32[]{:S(2)}, u32[]{:S(2)}) collective-permute-start(f32[64,2,4,1]{3,0,2,1:T(8,128)S(1)} %get-tuple-element.42), channel_id=1, source_target_pairs={{0,1},{1,2},{2,3},{4,5},{5,6},{6,7},{8,9},{9,10},{10,11},{12,13},{... | collective-permute-start | bytes 6152 | tf_op jit(solution)/shard_map/ppermute | solution.py:21
  82.2 9.0 %collective-permute-start.12 = (f32[64,2,4,1]{3,0,2,1:T(8,128)S(1)}, f32[64,2,4,1]{3,0,2,1:T(8,128)S(1)}, u32[]{:S(2)}, u32[]{:S(2)}) collective-permute-start(f32[64,2,4,1]{3,0,2,1:T(8,128)S(1)} %get-tuple-element.43), channel_id=1, source_target_pairs={{1,0},{2,1},{3,2},{5,4},{6,5},{7,6},{9,8},{10,9},{11,10},{13,12},{... | collective-permute-start | bytes 6152 | tf_op jit(solution)/shard_map/ppermute | solution.py:24
  105.5 9.0 %collective-permute-start.15 = (f32[64,2,4,1]{3,0,2,1:T(8,128)S(1)}, f32[64,2,4,1]{3,0,2,1:T(8,128)S(1)}, u32[]{:S(2)}, u32[]{:S(2)}) collective-permute-start(f32[64,2,4,1]{3,0,2,1:T(8,128)S(1)} %get-tuple-element.40), channel_id=1, source_target_pairs={{0,1},{1,2},{2,3},{4,5},{5,6},{6,7},{8,9},{9,10},{10,11},{12,13},{... | collective-permute-start | bytes 6152 | tf_op jit(solution)/shard_map/ppermute | solution.py:21
  107.7 9.3 %collective-permute-start.16 = (f32[64,2,4,1]{3,0,2,1:T(8,128)S(1)}, f32[64,2,4,1]{3,0,2,1:T(8,128)S(1)}, u32[]{:S(2)}, u32[]{:S(2)}) collective-permute-start(f32[64,2,4,1]{3,0,2,1:T(8,128)S(1)} %get-tuple-element.41), channel_id=1, source_target_pairs={{1,0},{2,1},{3,2},{5,4},{6,5},{7,6},{9,8},{10,9},{11,10},{13,12},{... | collective-permute-start | bytes 6152 | tf_op jit(solution)/shard_map/ppermute | solution.py:24
  122.2 11.4 %collective-permute-start.17 = (f32[64,2,2,128]{3,0,2,1:T(8,128)S(1)}, f32[64,2,2,128]{3,0,2,1:T(8,128)S(1)}, u32[]{:S(2)}, u32[]{:S(2)}) collective-permute-start(f32[64,2,2,128]{3,0,2,1:T(8,128)S(1)} %get-tuple-element.21), channel_id=1, source_target_pairs={{0,128},{1,129},{2,130},{3,131},{4,132},{5,133},{6,134},{7,135},{8... | collective-permute-start | bytes 393224 | tf_op jit(solution)/shard_map/ppermute | solution.py:32
  141.0 9.0 %collective-permute-start.20 = (f32[64,2,4,1]{3,0,2,1:T(8,128)S(1)}, f32[64,2,4,1]{3,0,2,1:T(8,128)S(1)}, u32[]{:S(2)}, u32[]{:S(2)}) collective-permute-start(f32[64,2,4,1]{3,0,2,1:T(8,128)S(1)} %get-tuple-element.38), channel_id=1, source_target_pairs={{0,1},{1,2},{2,3},{4,5},{5,6},{6,7},{8,9},{9,10},{10,11},{12,13},{... | collective-permute-start | bytes 6152 | tf_op jit(solution)/shard_map/ppermute | solution.py:21
  143.2 9.3 %collective-permute-start.21 = (f32[64,2,4,1]{3,0,2,1:T(8,128)S(1)}, f32[64,2,4,1]{3,0,2,1:T(8,128)S(1)}, u32[]{:S(2)}, u32[]{:S(2)}) collective-permute-start(f32[64,2,4,1]{3,0,2,1:T(8,128)S(1)} %get-tuple-element.39), channel_id=1, source_target_pairs={{1,0},{2,1},{3,2},{5,4},{6,5},{7,6},{9,8},{10,9},{11,10},{13,12},{... | collective-permute-start | bytes 6152 | tf_op jit(solution)/shard_map/ppermute | solution.py:24
  166.6 9.0 %collective-permute-start.24 = (f32[64,2,4,1]{3,0,2,1:T(8,128)S(1)}, f32[64,2,4,1]{3,0,2,1:T(8,128)S(1)}, u32[]{:S(2)}, u32[]{:S(2)}) collective-permute-start(f32[64,2,4,1]{3,0,2,1:T(8,128)S(1)} %get-tuple-element.36), channel_id=1, source_target_pairs={{0,1},{1,2},{2,3},{4,5},{5,6},{6,7},{8,9},{9,10},{10,11},{12,13},{... | collective-permute-start | bytes 6152 | tf_op jit(solution)/shard_map/ppermute | solution.py:21
  168.5 9.0 %collective-permute-start.25 = (f32[64,2,4,1]{3,0,2,1:T(8,128)S(1)}, f32[64,2,4,1]{3,0,2,1:T(8,128)S(1)}, u32[]{:S(2)}, u32[]{:S(2)}) collective-permute-start(f32[64,2,4,1]{3,0,2,1:T(8,128)S(1)} %get-tuple-element.37), channel_id=1, source_target_pairs={{1,0},{2,1},{3,2},{5,4},{6,5},{7,6},{9,8},{10,9},{11,10},{13,12},{... | collective-permute-start | bytes 6152 | tf_op jit(solution)/shard_map/ppermute | solution.py:24
  218.2 9.1 %collective-permute-start.33 = (f32[64,2,4,1]{3,0,2,1:T(8,128)S(1)}, f32[64,2,4,1]{3,0,2,1:T(8,128)S(1)}, u32[]{:S(2)}, u32[]{:S(2)}) collective-permute-start(f32[64,2,4,1]{3,0,2,1:T(8,128)S(1)} %get-tuple-element.33), channel_id=1, source_target_pairs={{1,0},{2,1},{3,2},{5,4},{6,5},{7,6},{9,8},{10,9},{11,10},{13,12},{... | collective-permute-start | bytes 6152 | tf_op jit(solution)/shard_map/ppermute | solution.py:24
  231.9 11.5 %collective-permute-start.34 = (f32[64,2,2,128]{3,0,2,1:T(8,128)S(1)}, f32[64,2,2,128]{3,0,2,1:T(8,128)S(1)}, u32[]{:S(2)}, u32[]{:S(2)}) collective-permute-start(f32[64,2,2,128]{3,0,2,1:T(8,128)S(1)} %bitcast.1716), channel_id=1, source_target_pairs={{128,0},{129,1},{130,2},{131,3},{132,4},{133,5},{134,6},{135,7},{1... | collective-permute-start | bytes 393224 | tf_op jit(solution)/shard_map/ppermute | solution.py:32
  254.8 9.3 %collective-permute-start.38 = (f32[64,2,4,1]{3,0,2,1:T(8,128)S(1)}, f32[64,2,4,1]{3,0,2,1:T(8,128)S(1)}, u32[]{:S(2)}, u32[]{:S(2)}) collective-permute-start(f32[64,2,4,1]{3,0,2,1:T(8,128)S(1)} %get-tuple-element.29), channel_id=1, source_target_pairs={{1,0},{2,1},{3,2},{5,4},{6,5},{7,6},{9,8},{10,9},{11,10},{13,12},{... | collective-permute-start | bytes 6152 | tf_op jit(solution)/shard_map/ppermute | solution.py:24
  276.3 9.0 %collective-permute-start.41 = (f32[64,2,4,1]{3,0,2,1:T(8,128)S(1)}, f32[64,2,4,1]{3,0,2,1:T(8,128)S(1)}, u32[]{:S(2)}, u32[]{:S(2)}) collective-permute-start(f32[64,2,4,1]{3,0,2,1:T(8,128)S(1)} %get-tuple-element.26), channel_id=1, source_target_pairs={{0,1},{1,2},{2,3},{4,5},{5,6},{6,7},{8,9},{9,10},{10,11},{12,13},{... | collective-permute-start | bytes 6152 | tf_op jit(solution)/shard_map/ppermute | solution.py:21
  278.4 9.3 %collective-permute-start.42 = (f32[64,2,4,1]{3,0,2,1:T(8,128)S(1)}, f32[64,2,4,1]{3,0,2,1:T(8,128)S(1)}, u32[]{:S(2)}, u32[]{:S(2)}) collective-permute-start(f32[64,2,4,1]{3,0,2,1:T(8,128)S(1)} %get-tuple-element.27), channel_id=1, source_target_pairs={{1,0},{2,1},{3,2},{5,4},{6,5},{7,6},{9,8},{10,9},{11,10},{13,12},{... | collective-permute-start | bytes 6152 | tf_op jit(solution)/shard_map/ppermute | solution.py:24
  292.3 11.6 %collective-permute-start.43 = (f32[64,2,2,128]{3,0,2,1:T(8,128)S(1)}, f32[64,2,2,128]{3,0,2,1:T(8,128)S(1)}, u32[]{:S(2)}, u32[]{:S(2)}) collective-permute-start(f32[64,2,2,128]{3,0,2,1:T(8,128)S(1)} %bitcast.1715), channel_id=1, source_target_pairs={{128,0},{129,1},{130,2},{131,3},{132,4},{133,5},{134,6},{135,7},{1... | collective-permute-start | bytes 393224 | tf_op jit(solution)/shard_map/ppermute | solution.py:32
  335.1 342.8 %all-reduce.17.cloned.1.call-start = ((), (), s32[]{:S(2)}) async-start(), calls=%async_computation.1 | async-start | bytes 3538944 | tf_op jit(solution)/shard_map/psum | solution.py:10
  344.0 83.6 %collective-permute-start.50 = (f32[64,2,4,1]{3,0,2,1:T(8,128)S(1)}, f32[64,2,4,1]{3,0,2,1:T(8,128)S(1)}, u32[]{:S(2)}, u32[]{:S(2)}) collective-permute-start(f32[64,2,4,1]{3,0,2,1:T(8,128)S(1)} %get-tuple-element.22), channel_id=1, source_target_pairs={{0,1},{1,2},{2,3},{4,5},{5,6},{6,7},{8,9},{9,10},{10,11},{12,13},{... | collective-permute-start | bytes 6152 | tf_op jit(solution)/shard_map/ppermute | solution.py:21
  345.9 81.6 %collective-permute-start.51 = (f32[64,2,4,1]{3,0,2,1:T(8,128)S(1)}, f32[64,2,4,1]{3,0,2,1:T(8,128)}, u32[]{:S(2)}, u32[]{:S(2)}) collective-permute-start(f32[64,2,4,1]{3,0,2,1:T(8,128)S(1)} %get-tuple-element.23), channel_id=1, source_target_pairs={{1,0},{2,1},{3,2},{5,4},{6,5},{7,6},{9,8},{10,9},{11,10},{13,12},{... | collective-permute-start | bytes 6152 | tf_op jit(solution)/shard_map/ppermute | solution.py:24
  (34 other events, 371.5 us)
Sparse Core Ops, SparseCore 0:
  335.3 284.1 all-reduce.14
  622.0 55.9 all-reduce.16
